TPU v7x, 512 devices: a whole 4x8x8 slice. The times are simulated.
512 devices in a mesh: row: 16 (over x, y_lo), col: 16 (over z, core), dp: 2 (over y_hi).
Axes of the slice: x: 4, y: 8 (y_hi: 2, y_lo: 4; y = y_hi * 4 + y_lo), z: 8, core: 2. Of those that a mesh axis runs over, the one named last changes fastest.
Arguments:
- grad_output: bfloat16 [2, 2048, 8192], P('dp', 'col', 'row'), may hold values from -0.09375 to 0.09375
- block_input: bfloat16 [2, 2048, 8192], P('dp', 'col', 'row'), may hold values from -6 to 6
- query_branch: bfloat16 [2, 2048, 8192], P('dp', 'row', 'col'), may hold values from -6 to 6
- key_branch: bfloat16 [2, 2048, 8192], P('dp', 'row', 'col'), may hold values from -6 to 6
- value_branch: bfloat16 [2, 2048, 8192], P('dp', 'row', 'col'), may hold values from -6 to 6
- out_weight: bfloat16 [8192, 8192], P('row', 'col'), may hold values from -0.0625 to 0.0625
- filters: float32 [512, 128], P('col'), may hold values from -0.5 to 0.5
Outputs:
- out_weight_grad: float32 [8192, 8192], P('row', 'col')
- value_weight_grad: float32 [8192, 8192], P('col', 'row')
- filter_grad: float32 [512, 128], P('col')
All inputs are finite; a program needn't handle non-finite values.
Results may differ from a plain program's by a relative error of at most 0.0029.
Values may be sent and summed in bfloat16 or wider, within the bound.
A program may use at most 128 MiB of HBM per device.

v0:
```python
import jax
import jax.numpy as jnp
from jax import lax
from jax.sharding import PartitionSpec as P

highest = lax.Precision.HIGHEST


def toeplitz(taps, tok_rows, causal):
    filter_len = taps.shape[1]
    out_pos = lax.broadcasted_iota(jnp.int32, (tok_rows, tok_rows + filter_len), 0)
    in_pos = lax.broadcasted_iota(jnp.int32, (tok_rows, tok_rows + filter_len), 1)
    lagged = out_pos + filter_len - in_pos if causal else in_pos - out_pos
    inside = (lagged >= 0) & (lagged < filter_len)
    picked = jnp.take(taps, jnp.clip(lagged, 0, filter_len - 1), axis=1)
    return jnp.where(inside[None], picked, 0.0)


def grouped_apply(table, signal, groups):
    blocks, extent, channels = signal.shape
    split = signal.reshape(blocks, extent, groups, channels // groups)
    result = jnp.einsum("gts,bsgc->btgc", table, split, precision=highest)
    return result.reshape(blocks, table.shape[1], channels)


def taps_partial(delta_mix, mixed_ext, groups, filter_len):
    blocks, tok_rows, channels = delta_mix.shape
    left_side = delta_mix.reshape(blocks, tok_rows, groups, channels // groups)
    right_side = mixed_ext.reshape(blocks, tok_rows + filter_len, groups, channels // groups)
    products = jnp.einsum("btgc,bsgc->gts", left_side, right_side, precision=highest)
    extent = tok_rows + filter_len
    flipped = products[:, :, ::-1]
    padded = jnp.pad(flipped, ((0, 0), (0, 0), (0, tok_rows)))
    flat_rows = padded.reshape(groups, -1)[:, : tok_rows * (extent + tok_rows - 1)]
    skewed = flat_rows.reshape(groups, tok_rows, extent + tok_rows - 1)
    column_sums = jnp.sum(skewed, axis=1)
    return column_sums[:, tok_rows - 1 : tok_rows - 1 + filter_len]


def local(grad_output, block_input, query_branch, key_branch, value_branch, out_weight, filters):
    filter_len = filters.shape[1]
    groups = filters.shape[0]
    tok_rows = query_branch.shape[1]
    channels = query_branch.shape[2]
    grads_all, inputs_all = (
        lax.all_gather(grad_output[0], "col", axis=0, tiled=True),
        lax.all_gather(block_input[0], "col", axis=0, tiled=True),
    )
    row_devices = lax.axis_size("row")
    sub_width = channels // row_devices
    delta_turned = lax.psum_scatter(
        lax.dot_general(
            out_weight, grads_all, (((0,), (1,)), ((), ())), preferred_element_type=jnp.float32
        ),
        "row",
        scatter_dimension=0,
        tiled=True,
    )
    queries, keys_here, values_here = (
        lax.all_to_all(query_branch[0], "row", split_axis=1, concat_axis=0, tiled=True),
        lax.all_to_all(key_branch[0], "row", split_axis=1, concat_axis=0, tiled=True),
        lax.all_to_all(value_branch[0], "row", split_axis=1, concat_axis=0, tiled=True),
    )
    delta_out = delta_turned.T
    local_groups = sub_width // (channels // groups)
    first_group = lax.axis_index("row") * local_groups
    my_taps = lax.dynamic_slice_in_dim(filters, first_group, local_groups, 0)
    mixed = keys_here.astype(jnp.float32) * values_here.astype(jnp.float32)
    mixed_blocks = mixed.reshape(row_devices, tok_rows, sub_width)
    earlier = jnp.concatenate(
        [
            jnp.zeros((1, filter_len, sub_width), jnp.float32),
            mixed_blocks[:-1, tok_rows - filter_len :],
        ],
        axis=0,
    )
    mixed_ext = jnp.concatenate([earlier, mixed_blocks], axis=1)
    conv_out = grouped_apply(toeplitz(my_taps, tok_rows, True), mixed_ext, local_groups).reshape(
        -1, sub_width
    )
    gated = (queries.astype(jnp.float32) * conv_out).astype(jnp.bfloat16)
    delta_mix = delta_out * queries.astype(jnp.float32)
    delta_blocks = delta_mix.reshape(row_devices, tok_rows, sub_width)
    later_part = jnp.concatenate(
        [delta_blocks[1:, :filter_len], jnp.zeros((1, filter_len, sub_width), jnp.float32)], axis=0
    )
    delta_ext = jnp.concatenate([delta_blocks, later_part], axis=1)
    delta_conv = grouped_apply(toeplitz(my_taps, tok_rows, False), delta_ext, local_groups).reshape(
        -1, sub_width
    )
    delta_value = (delta_conv * keys_here.astype(jnp.float32)).astype(jnp.bfloat16)
    my_terms = taps_partial(delta_blocks, mixed_ext, local_groups, filter_len)
    taps_local = lax.dynamic_update_slice_in_dim(
        jnp.zeros(filters.shape, jnp.float32), my_terms, first_group, 0
    )
    gated_all, value_all = (
        lax.all_gather(gated, "row", axis=1, tiled=True),
        lax.all_gather(delta_value, "row", axis=1, tiled=True),
    )
    out_grad = lax.dot_general(
        grads_all, gated_all, (((0,), (0,)), ((), ())), preferred_element_type=jnp.float32
    )
    value_grad = lax.dot_general(
        value_all, inputs_all, (((0,), (0,)), ((), ())), preferred_element_type=jnp.float32
    )
    out_grad, value_grad = lax.psum((out_grad, value_grad), "dp")
    taps_total = lax.psum(taps_local, ("row", "dp"))
    return (out_grad, value_grad, taps_total)


def solution(mesh):
    in_specs = (
        P("dp", "col", "row"),
        P("dp", "col", "row"),
        P("dp", "row", "col"),
        P("dp", "row", "col"),
        P("dp", "row", "col"),
        P("row", "col"),
        P("col", None),
    )
    out_specs = (P("row", "col"), P("col", "row"), P("col", None))
    return jax.shard_map(local, mesh=mesh, in_specs=in_specs, out_specs=out_specs, check_vma=False)
```

profile of v0, /device:TPU:64, one launch (start us, length us, event | category | flops | bytes accessed | tf_op | source)
XLA Modules:
  0.0 689.4 jit_solution(379694975442089937)
XLA Ops:
  7.2 0.7 all-gather.11.cloned.1.call-update
  8.0 48.5 %all-gather.11.cloned.1.call-done = bf16[1,2048,512]{2,1,0:T(8,128)(2,1)} async-done(((bf16[1,128,512]{2,1,0:T(8,128)(2,1)}), bf16[1,2048,512]{2,1,0:T(8,128)(2,1)}) %all-gather.11.cloned.1.call-update) | async-done | bytes 2097168 | tf_op jit(solution)/shard_map/all_gather | solution.py:46
  56.5 4.8 fusion.2
  61.4 0.9 copy-done.2
  62.2 0.8 copy.40
  63.0 7.1 %all-to-all-start.2 = ((bf16[128,16,32]{0,2,1:T(8,128)(2,1)}), bf16[128,16,32]{0,2,1:T(8,128)(2,1)S(1)}, u32[]{:S(2)}, u32[]{:S(2)}) async-start(bf16[128,16,32]{0,2,1:T(8,128)(2,1)} %bitcast.4), calls=%async_computation.2 | async-start | bytes 262144 | tf_op jit(solution)/shard_map/all_to_all | solution.py:62
  70.4 0.7 constant_dynamic-slice_fusion
  71.1 0.8 copy.38
  71.9 109.0 %gather_fusion = f32[32768,2]{1,0:T(8,128)} fusion(f32[2,128]{0,1:T(8,128)S(1)} %copy.62, s32[32768]{0:T(1024)S(1)} %broadcast_clamp_fusion.1), kind=kCustom, calls=%fused_computation.clone | custom fusion | bytes 655360 | tf_op jit(solution)/shard_map/jit(_take)/gather | solution.py:15
  180.9 10.0 %copy.46 = f32[128,256,2]{1,0,2:T(8,128)S(1)} copy(f32[128,256,2]{2,1,0:T(8,128)} %bitcast.113) | data formatting | bytes 524288 | tf_op jit(solution)/shard_map/jit(_take)/gather | solution.py:15
  190.9 0.8 copy.36
  191.9 7.5 %all-to-all-start.1 = ((bf16[128,16,32]{0,2,1:T(8,128)(2,1)}), bf16[128,16,32]{0,2,1:T(8,128)(2,1)S(1)}, u32[]{:S(2)}, u32[]{:S(2)}) async-start(bf16[128,16,32]{0,2,1:T(8,128)(2,1)} %bitcast.2), calls=%async_computation.1 | async-start | bytes 262144 | tf_op jit(solution)/shard_map/all_to_all | solution.py:61
  199.4 8.4 %all-to-all-done.1 = bf16[128,16,32]{0,2,1:T(8,128)(2,1)S(1)} async-done(((bf16[128,16,32]{0,2,1:T(8,128)(2,1)}), bf16[128,16,32]{0,2,1:T(8,128)(2,1)S(1)}, u32[]{:S(2)}, u32[]{:S(2)}) %all-to-all-start.1) | async-done | bytes 131104 | tf_op jit(solution)/shard_map/all_to_all | solution.py:61
  207.8 3.5 all-to-all-start
  211.7 0.6 convolution_bitcast_fusion.2
  212.4 7.3 %all-to-all-done = bf16[128,16,32]{0,2,1:T(8,128)(2,1)S(1)} async-done(((bf16[128,16,32]{0,2,1:T(8,128)(2,1)}), bf16[128,16,32]{0,2,1:T(8,128)(2,1)S(1)}, u32[]{:S(2)}, u32[]{:S(2)}) %all-to-all-start) | async-done | bytes 131104 | tf_op jit(solution)/shard_map/all_to_all | solution.py:60
  219.6 1.7 bitcast_multiply_fusion.2
  221.4 0.5 all-gather.13.cloned.1.call-update
  222.2 109.0 %gather_fusion.1 = f32[32768,2]{1,0:T(8,128)} fusion(f32[2,128]{0,1:T(8,128)S(1)} %copy.62, s32[32768]{0:T(1024)S(1)} %broadcast_clamp_fusion), kind=kCustom, calls=%fused_computation.1.clone | custom fusion | bytes 655360 | tf_op jit(solution)/shard_map/jit(_take)/gather | solution.py:15
  331.2 10.1 %copy.51 = f32[128,256,2]{1,0,2:T(8,128)S(1)} copy(f32[128,256,2]{2,1,0:T(8,128)} %bitcast.112) | data formatting | bytes 524288 | tf_op jit(solution)/shard_map/jit(_take)/gather | solution.py:15
  341.7 0.6 convolution_bitcast_fusion.1
  342.4 0.7 fusion.13
  343.2 4.5 fusion.6
  347.7 1.5 all-gather.13.cloned.1.call-done
  349.2 91.4 %all-gather.9.cloned.1.call-done = bf16[2048,512]{0,1:T(8,128)(2,1)} async-done(((bf16[2048,32]{0,1:T(8,128)(2,1)}), bf16[2048,512]{0,1:T(8,128)(2,1)}) %all-gather.9.cloned.1.call-update) | async-done | bytes 2097168 | tf_op jit(solution)/shard_map/all_gather | solution.py:98
  440.6 4.4 fusion
  445.1 0.8 convolution_bitcast_fusion
  445.9 0.4 rev.3
  446.7 0.6 reshape.76
  447.4 231.5 %psum.23 = f32[32,128]{1,0:T(8,128)} all-reduce(f32[32,128]{1,0:T(8,128)S(1)} %slice_dynamic-update-slice_fusion), channel_id=1, replica_groups=mesh['row'=16,'col'=16,'dp'=2] {'row','dp'}, use_global_device_ids=true, to_apply=%region_4.6 | all-reduce | flops 4096 | bytes 32768 | tf_op jit(solution)/shard_map/psum | solution.py:107
  678.9 2.6 copy.54
  681.5 1.0 copy.88
  (55 shorter events, 2.3 us)
Async XLA Ops:
  7.2 49.3 %copy-start = (bf16[512,512]{1,0:T(8,128)(2,1)S(1)}, bf16[512,512]{1,0:T(8,128)(2,1)}, u32[]{:S(2)}) copy-start(bf16[512,512]{1,0:T(8,128)(2,1)} %param.14) | copy-start | bytes 1572868
  7.2 49.3 %all-gather.11.cloned.1.call-start = ((), (), s32[]{:S(2)}) async-start(), calls=%async_computation.7 | async-start | bytes 2228224 | tf_op jit(solution)/shard_map/all_gather | solution.py:46
  7.9 211.7 %reduce-scatter.2.cloned.1.call-start = ((), (), s32[]{:S(2)}) async-start(), calls=%async_computation.5 | async-start | bytes 4456448 | tf_op jit(solution)/shard_map/reduce_scatter | solution.py:51
  61.3 0.9 copy-start.2
  61.3 9.7 %copy-start.3 = (bf16[1,128,512]{2,1,0:T(8,128)(2,1)S(1)}, bf16[1,128,512]{2,1,0:T(8,128)(2,1)}, u32[]{:S(2)}) copy-start(bf16[1,128,512]{2,1,0:T(8,128)(2,1)} %param.12) | copy-start | bytes 393220
  63.0 128.9 %all-to-all-start.2 = ((bf16[128,16,32]{0,2,1:T(8,128)(2,1)}), bf16[128,16,32]{0,2,1:T(8,128)(2,1)S(1)}, u32[]{:S(2)}, u32[]{:S(2)}) async-start(bf16[128,16,32]{0,2,1:T(8,128)(2,1)} %bitcast.4), calls=%async_computation.2 | async-start | bytes 262144 | tf_op jit(solution)/shard_map/all_to_all | solution.py:62
  180.9 10.0 %copy-start.4 = (bf16[1,128,512]{2,1,0:T(8,128)(2,1)S(1)}, bf16[1,128,512]{2,1,0:T(8,128)(2,1)}, u32[]{:S(2)}) copy-start(bf16[1,128,512]{2,1,0:T(8,128)(2,1)} %param.11) | copy-start | bytes 393220
  191.9 15.9 %all-to-all-start.1 = ((bf16[128,16,32]{0,2,1:T(8,128)(2,1)}), bf16[128,16,32]{0,2,1:T(8,128)(2,1)S(1)}, u32[]{:S(2)}, u32[]{:S(2)}) async-start(bf16[128,16,32]{0,2,1:T(8,128)(2,1)} %bitcast.2), calls=%async_computation.1 | async-start | bytes 262144 | tf_op jit(solution)/shard_map/all_to_all | solution.py:61
  207.8 11.9 %all-to-all-start = ((bf16[128,16,32]{0,2,1:T(8,128)(2,1)}), bf16[128,16,32]{0,2,1:T(8,128)(2,1)S(1)}, u32[]{:S(2)}, u32[]{:S(2)}) async-start(bf16[128,16,32]{0,2,1:T(8,128)(2,1)} %bitcast), calls=%async_computation | async-start | bytes 262144 | tf_op jit(solution)/shard_map/all_to_all | solution.py:60
  211.3 131.9 %all-gather.7.cloned.1.call-start = ((), (), s32[]{:S(2)}) async-start(), calls=%async_computation.4 | async-start | bytes 2228224 | tf_op jit(solution)/shard_map/all_gather | solution.py:97
  221.4 127.9 %all-gather.13.cloned.1.call-start = ((), (), s32[]{:S(2)}) async-start(), calls=%async_computation.8 | async-start | bytes 2228224 | tf_op jit(solution)/shard_map/all_gather | solution.py:47
  222.0 218.7 %all-gather.9.cloned.1.call-start = ((), (), s32[]{:S(2)}) async-start(), calls=%async_computation.6 | async-start | bytes 2228224 | tf_op jit(solution)/shard_map/all_gather | solution.py:98
  343.2 335.8 %all-reduce.6.cloned.1.call-start = ((), (), s32[]{:S(2)}) async-start(), calls=%async_computation.9 | async-start | bytes 4194304 | tf_op jit(solution)/shard_map/psum | solution.py:106
  678.9 2.6 copy-start.1
Sparse Core Ops, SparseCore 0:
  10.1 46.3 all-gather.10
  61.5 105.1 reduce-scatter.1
  221.5 84.2 all-gather.6
  307.8 41.4 all-gather.12
  351.7 88.8 all-gather.8
  445.2 122.4 all-reduce.5
where the time goes:
time: 690 us; the launch traced here: 689 us
  local copies, waits for them, and re-layouts  248 us (36%)
  blocking collectives  232 us (34%)
  waiting for transfers between devices  158 us (23%)
  starting transfers between devices  18.4 us (3%)
  matrix products  15.8 us (2%)
  between operations  14.4 us (2%)
    gather x4, local copies, waits for them, and re-layouts, toeplitz(): picked = jnp.take(taps, jnp.clip(lagged, 0, filter_len - 1), axis=1)  238 us
    psum x1, blocking collectives, local(): taps_total = lax.psum(taps_local, ('row', 'dp'))  232 us
    all_gather x1, waiting for transfers between devices, local(): lax.all_gather(delta_value, 'row', axis=1, tiled=True)  91.4 us
    all_gather x1, waiting for transfers between devices, local(): lax.all_gather(grad_output[0], 'col', axis=0, tiled=True)  48.5 us
  transfers between devices with their start and end apart: 9, of which 5 were waited for; matrix products, arithmetic and copies ran while one was open for 36% of the time, Pallas kernels for 0%

commit v1 on v0

--- a/solution.py
+++ b/solution.py
@@ -104,7 +104,8 @@
         value_all, inputs_all, (((0,), (0,)), ((), ())), preferred_element_type=jnp.float32
     )
     out_grad, value_grad = lax.psum((out_grad, value_grad), "dp")
-    taps_total = lax.psum(taps_local, ("row", "dp"))
+    parts = lax.all_gather(taps_local, ("row", "dp"))
+    taps_total = jnp.sum(parts, axis=0)
     return (out_grad, value_grad, taps_total)
 
 

time: 690 us -> 631 us (0.914)
  blocking collectives: 232 us -> 171 us
    psum x1 -> x0, blocking collectives: 232 us -> none  [local(): taps_total = lax.psum(taps_local, ('row', 'dp'))]
    all_gather x0 -> x1, blocking collectives: none -> 171 us  [local(): parts = lax.all_gather(taps_local, ('row', 'dp'))]
  transfers between devices with their start and end apart: 9 -> 9, of which waited for: 5 -> 5; matrix products, arithmetic and copies ran while one was open for 36% -> 40% of each run, Pallas kernels for 0% -> 0%
where the time goes in v1:
time: 631 us; the launch traced here: 630 us
  local copies, waits for them, and re-layouts  248 us (39%)
  blocking collectives  171 us (27%)
  waiting for transfers between devices  158 us (25%)
  starting transfers between devices  18.4 us (3%)
  matrix products  15.8 us (3%)
  between operations  14.4 us (2%)
    gather x4, local copies, waits for them, and re-layouts, toeplitz(): picked = jnp.take(taps, jnp.clip(lagged, 0, filter_len - 1), axis=1)  238 us
    all_gather x1, blocking collectives, local(): parts = lax.all_gather(taps_local, ('row', 'dp'))  171 us
    all_gather x1, waiting for transfers between devices, local(): lax.all_gather(delta_value, 'row', axis=1, tiled=True)  91.4 us
    all_gather x1, waiting for transfers between devices, local(): lax.all_gather(grad_output[0], 'col', axis=0, tiled=True)  48.5 us
  transfers between devices with their start and end apart: 9, of which 5 were waited for; matrix products, arithmetic and copies ran while one was open for 40% of the time, Pallas kernels for 0%

profile of v1, /device:TPU:64, one launch (start us, length us, event | category | flops | bytes accessed | tf_op | source)
XLA Modules:
  0.0 629.9 jit_solution(17899778265998381966)
XLA Ops:
  7.2 0.7 all-gather.11.cloned.1.call-update
  8.0 48.5 %all-gather.11.cloned.1.call-done = bf16[1,2048,512]{2,1,0:T(8,128)(2,1)} async-done(((bf16[1,128,512]{2,1,0:T(8,128)(2,1)}), bf16[1,2048,512]{2,1,0:T(8,128)(2,1)}) %all-gather.11.cloned.1.call-update) | async-done | bytes 2097168 | tf_op jit(solution)/shard_map/all_gather | solution.py:46
  56.5 4.8 fusion.2
  61.4 0.9 copy-done.2
  62.2 0.8 copy.59
  63.0 7.1 %all-to-all-start.2 = ((bf16[128,16,32]{0,2,1:T(8,128)(2,1)}), bf16[128,16,32]{0,2,1:T(8,128)(2,1)S(1)}, u32[]{:S(2)}, u32[]{:S(2)}) async-start(bf16[128,16,32]{0,2,1:T(8,128)(2,1)} %bitcast.4), calls=%async_computation.2 | async-start | bytes 262144 | tf_op jit(solution)/shard_map/all_to_all | solution.py:62
  70.4 0.7 constant_dynamic-slice_fusion
  71.1 0.8 copy.57
  71.9 109.0 %gather_fusion = f32[32768,2]{1,0:T(8,128)} fusion(f32[2,128]{0,1:T(8,128)S(1)} %copy.81, s32[32768]{0:T(1024)S(1)} %broadcast_clamp_fusion.1), kind=kCustom, calls=%fused_computation.clone | custom fusion | bytes 655360 | tf_op jit(solution)/shard_map/jit(_take)/gather | solution.py:15
  180.9 10.0 %copy.65 = f32[128,256,2]{1,0,2:T(8,128)S(1)} copy(f32[128,256,2]{2,1,0:T(8,128)} %bitcast.117) | data formatting | bytes 524288 | tf_op jit(solution)/shard_map/jit(_take)/gather | solution.py:15
  190.9 0.8 copy.55
  191.9 7.5 %all-to-all-start.1 = ((bf16[128,16,32]{0,2,1:T(8,128)(2,1)}), bf16[128,16,32]{0,2,1:T(8,128)(2,1)S(1)}, u32[]{:S(2)}, u32[]{:S(2)}) async-start(bf16[128,16,32]{0,2,1:T(8,128)(2,1)} %bitcast.2), calls=%async_computation.1 | async-start | bytes 262144 | tf_op jit(solution)/shard_map/all_to_all | solution.py:61
  199.4 8.4 %all-to-all-done.1 = bf16[128,16,32]{0,2,1:T(8,128)(2,1)S(1)} async-done(((bf16[128,16,32]{0,2,1:T(8,128)(2,1)}), bf16[128,16,32]{0,2,1:T(8,128)(2,1)S(1)}, u32[]{:S(2)}, u32[]{:S(2)}) %all-to-all-start.1) | async-done | bytes 131104 | tf_op jit(solution)/shard_map/all_to_all | solution.py:61
  207.8 3.5 all-to-all-start
  211.7 0.6 convolution_bitcast_fusion.2
  212.4 7.3 %all-to-all-done = bf16[128,16,32]{0,2,1:T(8,128)(2,1)S(1)} async-done(((bf16[128,16,32]{0,2,1:T(8,128)(2,1)}), bf16[128,16,32]{0,2,1:T(8,128)(2,1)S(1)}, u32[]{:S(2)}, u32[]{:S(2)}) %all-to-all-start) | async-done | bytes 131104 | tf_op jit(solution)/shard_map/all_to_all | solution.py:60
  219.6 1.7 bitcast_multiply_fusion.2
  221.4 0.5 all-gather.13.cloned.1.call-update
  222.2 109.0 %gather_fusion.1 = f32[32768,2]{1,0:T(8,128)} fusion(f32[2,128]{0,1:T(8,128)S(1)} %copy.81, s32[32768]{0:T(1024)S(1)} %broadcast_clamp_fusion), kind=kCustom, calls=%fused_computation.1.clone | custom fusion | bytes 655360 | tf_op jit(solution)/shard_map/jit(_take)/gather | solution.py:15
  331.2 10.1 %copy.70 = f32[128,256,2]{1,0,2:T(8,128)S(1)} copy(f32[128,256,2]{2,1,0:T(8,128)} %bitcast.116) | data formatting | bytes 524288 | tf_op jit(solution)/shard_map/jit(_take)/gather | solution.py:15
  341.7 0.6 convolution_bitcast_fusion.1
  342.4 0.7 fusion.13
  343.2 4.5 fusion.6
  347.7 1.5 all-gather.13.cloned.1.call-done
  349.2 91.4 %all-gather.9.cloned.1.call-done = bf16[2048,512]{0,1:T(8,128)(2,1)} async-done(((bf16[2048,32]{0,1:T(8,128)(2,1)}), bf16[2048,512]{0,1:T(8,128)(2,1)}) %all-gather.9.cloned.1.call-update) | async-done | bytes 2097168 | tf_op jit(solution)/shard_map/all_gather | solution.py:98
  440.6 4.4 fusion
  445.1 0.8 convolution_bitcast_fusion
  446.7 0.6 reshape.78
  447.4 171.4 %all_gather.23 = f32[32,32,128]{2,1,0:T(8,128)S(1)} all-gather(f32[1,32,128]{2,1,0:T(8,128)S(1)} %fusion.41), channel_id=1, replica_groups=mesh['row'=16,'col'=16,'dp'=2] {'row','dp'}, dimensions={0}, use_global_device_ids=true | all-gather | bytes 540672 | tf_op jit(solution)/shard_map/all_gather | solution.py:107
  618.8 0.6 reduce_sum.19
  619.5 2.6 copy.73
  622.1 1.0 copy.107
  (56 shorter events, 2.7 us)
Async XLA Ops:
  7.2 49.3 %copy-start = (bf16[512,512]{1,0:T(8,128)(2,1)S(1)}, bf16[512,512]{1,0:T(8,128)(2,1)}, u32[]{:S(2)}) copy-start(bf16[512,512]{1,0:T(8,128)(2,1)} %param.14) | copy-start | bytes 1572868
  7.2 49.3 %all-gather.11.cloned.1.call-start = ((), (), s32[]{:S(2)}) async-start(), calls=%async_computation.7 | async-start | bytes 2228224 | tf_op jit(solution)/shard_map/all_gather | solution.py:46
  7.9 211.7 %reduce-scatter.2.cloned.1.call-start = ((), (), s32[]{:S(2)}) async-start(), calls=%async_computation.5 | async-start | bytes 4456448 | tf_op jit(solution)/shard_map/reduce_scatter | solution.py:51
  61.3 0.9 copy-start.2
  61.3 9.7 %copy-start.3 = (bf16[1,128,512]{2,1,0:T(8,128)(2,1)S(1)}, bf16[1,128,512]{2,1,0:T(8,128)(2,1)}, u32[]{:S(2)}) copy-start(bf16[1,128,512]{2,1,0:T(8,128)(2,1)} %param.12) | copy-start | bytes 393220
  63.0 128.9 %all-to-all-start.2 = ((bf16[128,16,32]{0,2,1:T(8,128)(2,1)}), bf16[128,16,32]{0,2,1:T(8,128)(2,1)S(1)}, u32[]{:S(2)}, u32[]{:S(2)}) async-start(bf16[128,16,32]{0,2,1:T(8,128)(2,1)} %bitcast.4), calls=%async_computation.2 | async-start | bytes 262144 | tf_op jit(solution)/shard_map/all_to_all | solution.py:62
  180.9 10.0 %copy-start.4 = (bf16[1,128,512]{2,1,0:T(8,128)(2,1)S(1)}, bf16[1,128,512]{2,1,0:T(8,128)(2,1)}, u32[]{:S(2)}) copy-start(bf16[1,128,512]{2,1,0:T(8,128)(2,1)} %param.11) | copy-start | bytes 393220
  191.9 15.9 %all-to-all-start.1 = ((bf16[128,16,32]{0,2,1:T(8,128)(2,1)}), bf16[128,16,32]{0,2,1:T(8,128)(2,1)S(1)}, u32[]{:S(2)}, u32[]{:S(2)}) async-start(bf16[128,16,32]{0,2,1:T(8,128)(2,1)} %bitcast.2), calls=%async_computation.1 | async-start | bytes 262144 | tf_op jit(solution)/shard_map/all_to_all | solution.py:61
  207.8 11.9 %all-to-all-start = ((bf16[128,16,32]{0,2,1:T(8,128)(2,1)}), bf16[128,16,32]{0,2,1:T(8,128)(2,1)S(1)}, u32[]{:S(2)}, u32[]{:S(2)}) async-start(bf16[128,16,32]{0,2,1:T(8,128)(2,1)} %bitcast), calls=%async_computation | async-start | bytes 262144 | tf_op jit(solution)/shard_map/all_to_all | solution.py:60
  211.3 131.9 %all-gather.7.cloned.1.call-start = ((), (), s32[]{:S(2)}) async-start(), calls=%async_computation.4 | async-start | bytes 2228224 | tf_op jit(solution)/shard_map/all_gather | solution.py:97
  221.4 127.9 %all-gather.13.cloned.1.call-start = ((), (), s32[]{:S(2)}) async-start(), calls=%async_computation.8 | async-start | bytes 2228224 | tf_op jit(solution)/shard_map/all_gather | solution.py:47
  222.0 218.7 %all-gather.9.cloned.1.call-start = ((), (), s32[]{:S(2)}) async-start(), calls=%async_computation.6 | async-start | bytes 2228224 | tf_op jit(solution)/shard_map/all_gather | solution.py:98
  343.2 276.3 %all-reduce.6.cloned.1.call-start = ((), (), s32[]{:S(2)}) async-start(), calls=%async_computation.9 | async-start | bytes 4194304 | tf_op jit(solution)/shard_map/psum | solution.py:106
  619.5 2.6 copy-start.1
Sparse Core Ops, SparseCore 0:
  10.1 46.3 all-gather.10
  61.5 105.1 reduce-scatter.1
  221.5 84.2 all-gather.6
  307.8 41.4 all-gather.12
  351.7 88.8 all-gather.8
  445.2 126.5 all-reduce.5
